TPU v7x, 512 devices: a whole 4x8x8 slice. The times are simulated.
512 devices in a mesh: region: 16 (over z, core), pos: 32 (over x, y).
Axes of the slice: x: 4, y: 8, z: 8, core: 2. Of those that a mesh axis runs over, the one named last changes fastest.
Arguments:
- object_tiles: bfloat16 [2, 2048, 4096], P(None, 'region', 'pos'), may hold values from -4.1875 to 4.1875
- probe: float32 [2, 4, 128, 128], replicated, may hold values from -3 to 3
- amplitudes: float32 [16, 128, 128, 128], P('region', 'pos'), may hold values from 0.3 to 6
- offsets: int32 [16, 2, 128], P('region', None, 'pos'), may hold values from 0 to 127
- counts: int32 [16, 32], P('region', 'pos'), may hold values from 1 to 4
Outputs:
- object_grad: float32 [2, 2048, 4096], P(None, 'region', 'pos')
- probe_grad: float32 [2, 4, 128, 128], replicated
All inputs are finite; a program needn't handle non-finite values.
Results may differ from a plain program's by a relative error of at most 0.0003.
Values may be sent and summed in bfloat16 or wider, within the bound.
A program may use at most 64 MiB of HBM per device.

v0:
```python
import math

import jax
import jax.numpy as jnp
from jax import lax
from jax.sharding import Mesh
from jax.sharding import PartitionSpec as P

REGION = ("region_0", "region_1")
POS = ("pos_0", "pos_1")


def passed_along(block, axis, distance):
    devices = range(lax.axis_size(axis))
    route = [(i - distance, i) for i in devices if i - distance in devices]
    return lax.ppermute(block, axis, route)


def padded_to(lines, count):
    spare = -lines.shape[0] % count
    if not spare:
        return lines
    return jnp.concatenate([lines, jnp.zeros((spare, *lines.shape[1:]), lines.dtype)])


def copy_for_each(shard, axis):
    copies = jnp.broadcast_to(shard, (lax.axis_size(axis), *shard.shape))
    return lax.all_to_all(copies, axis, split_axis=0, concat_axis=0, tiled=True)


def in_order(parts, dim):
    lengths = list(parts.shape[1:])
    lengths[dim] *= parts.shape[0]
    return jnp.moveaxis(parts, 0, dim).reshape(lengths)


def gather_axes(shard, axes, dim):
    far, near = axes
    initial = copy_for_each(shard, far)
    parts = jnp.swapaxes(copy_for_each(initial, near), 0, 1)
    return in_order(parts.reshape(-1, *shard.shape), dim)


def cut_along(shard, dim, count):
    before, after = (shard.shape[:dim], shard.shape[dim + 1 :])
    return jnp.moveaxis(shard.reshape(*before, count, -1, *after), dim, 0)


def sum_at_owner(shard, axis, dim):
    count = lax.axis_size(axis)
    parts = lax.all_to_all(cut_along(shard, dim, count), axis, 0, 0, tiled=True)
    return jnp.sum(parts, axis=0)


def sum_in_two_steps(shard, axes, dim):
    far, near = axes
    own = sum_at_owner(cut_along(shard, dim, lax.axis_size(far)), near, dim + 1)
    return jnp.sum(lax.all_to_all(own, far, 0, 0, tiled=True), axis=0)


def sum_by_parts(shard, axes):
    lines = shard.reshape(-1, shard.shape[-1])
    padded = padded_to(lines, lax.axis_size(axes[0]) * lax.axis_size(axes[1]))
    whole = gather_axes(sum_in_two_steps(padded, axes, 0), axes, 0)
    return lax.slice_in_dim(whole, 0, len(lines)).reshape(shard.shape)


def dft_tables(order):
    row_index_list = jnp.arange(order, dtype=jnp.int32)
    product = row_index_list[:, None] * row_index_list[None, :] % order
    angle = product.astype(jnp.float32) * (2.0 * math.pi / order)
    norm_factor = 1.0 / math.sqrt(order)
    return (jnp.cos(angle) * norm_factor, jnp.sin(angle) * norm_factor)


def both_sides(real_part, imag_part, cos_table, sin_table):
    high = lax.Precision.HIGHEST
    left_r = jnp.einsum("ab,mbc->mac", cos_table, real_part, precision=high) - jnp.einsum(
        "ab,mbc->mac", sin_table, imag_part, precision=high
    )
    left_i = jnp.einsum("ab,mbc->mac", cos_table, imag_part, precision=high) + jnp.einsum(
        "ab,mbc->mac", sin_table, real_part, precision=high
    )
    right_r = jnp.einsum("mab,bc->mac", left_r, cos_table, precision=high) - jnp.einsum(
        "mab,bc->mac", left_i, sin_table, precision=high
    )
    right_i = jnp.einsum("mab,bc->mac", left_i, cos_table, precision=high) + jnp.einsum(
        "mab,bc->mac", left_r, sin_table, precision=high
    )
    return (right_r, right_i)


def position_terms(obj_patch, probe, amplitude, cos_table, sin_table):
    exit_r = probe[0] * obj_patch[0][None] - probe[1] * obj_patch[1][None]
    exit_i = probe[0] * obj_patch[1][None] + probe[1] * obj_patch[0][None]
    far_r, far_i = both_sides(exit_r, exit_i, cos_table, -sin_table)
    intensity = jnp.sum(far_r * far_r + far_i * far_i, axis=0)
    factor = 1.0 - amplitude / jnp.sqrt(intensity + 1.0)
    back_r, back_i = both_sides(far_r * factor[None], far_i * factor[None], cos_table, sin_table)
    obj_r = jnp.sum(probe[0] * back_r + probe[1] * back_i, axis=0)
    obj_i = jnp.sum(probe[0] * back_i - probe[1] * back_r, axis=0)
    probe_r = obj_patch[0][None] * back_r + obj_patch[1][None] * back_i
    probe_i = obj_patch[0][None] * back_i - obj_patch[1][None] * back_r
    return (jnp.stack([obj_r, obj_i]), jnp.stack([probe_r, probe_i]))


def on_device(object_tiles, probe, amplitudes, offsets, counts):
    edge = probe.shape[2]
    slot_total = amplitudes.shape[1]
    below_own = passed_along(object_tiles, REGION, -1)
    left_pair = jnp.concatenate([object_tiles, below_own], axis=1)
    right_pair = passed_along(left_pair, POS, -1)
    window = jnp.concatenate([left_pair, right_pair], axis=2)
    window = window.astype(jnp.float32)
    cos_table, sin_table = dft_tables(edge)
    live_count = counts[0, 0]
    zero_index = jnp.zeros((), jnp.int32)

    def visit(slot_index, carry):
        grad_field, probe_sum = carry
        row0 = offsets[0, 0, slot_index]
        col0 = offsets[0, 1, slot_index]
        obj_patch = lax.dynamic_slice(window, (zero_index, row0, col0), (2, edge, edge))
        obj_term, probe_term = position_terms(
            obj_patch, probe, amplitudes[0, slot_index], cos_table, sin_table
        )
        weight = (slot_index < live_count).astype(jnp.float32)
        current = lax.dynamic_slice(grad_field, (zero_index, row0, col0), (2, edge, edge))
        grad_field = lax.dynamic_update_slice(
            grad_field, current + weight * obj_term, (zero_index, row0, col0)
        )
        return (grad_field, probe_sum + weight * probe_term)

    start = (jnp.zeros((2, 2 * edge, 2 * edge), jnp.float32), jnp.zeros(probe.shape, jnp.float32))
    grad_field, probe_sum = lax.fori_loop(0, slot_total, visit, start)
    from_above = passed_along(grad_field[:, edge:, :], REGION, 1)
    upper_grad = grad_field[:, :edge, :] + from_above
    from_left = passed_along(upper_grad[:, :, edge:], POS, 1)
    object_grad = upper_grad[:, :, :edge] + from_left
    scale = 1.0 / math.sqrt(lax.axis_size(REGION) * lax.axis_size(POS) * slot_total)
    probe_grad = sum_by_parts(probe_sum, (("region_0", "region_1"), ("pos_0", "pos_1"))) * scale
    return (object_grad, probe_grad)


def solution(mesh):
    finer = Mesh(mesh.devices.reshape(8, 2, 4, 8), ("region_0", "region_1", "pos_0", "pos_1"))
    return jax.shard_map(
        on_device,
        mesh=finer,
        in_specs=(
            P(None, REGION, POS),
            P(),
            P(REGION, POS, None, None),
            P(REGION, None, POS),
            P(REGION, POS),
        ),
        out_specs=(P(None, REGION, POS), P()),
        check_vma=False,
    )
```

profile of v0, /device:TPU:7, one launch (start us, length us, event | category | flops | bytes accessed | tf_op | source)
XLA Modules:
  0.0 179.6 jit_solution(16546141705258976519)
XLA Ops:
  0.6 2.6 %collective-permute-start = (bf16[2,128,128]{2,1,0:T(8,128)(2,1)}, bf16[2,128,128]{2,1,0:T(8,128)(2,1)S(1)}, u32[]{:S(2)}, u32[]{:S(2)}) collective-permute-start(bf16[2,128,128]{2,1,0:T(8,128)(2,1)} %param.7), channel_id=1, source_target_pairs={{32,0},{64,32},{96,64},{128,96},{160,128},{192,160},{224,192},{256... | collective-permute-start | bytes 196616 | tf_op jit(solution)/shard_map/ppermute | solution.py:16
  3.2 0.8 constant_dynamic-update-slice_fusion.1
  4.1 3.3 %collective-permute-done = bf16[2,128,128]{2,1,0:T(8,128)(2,1)S(1)} collective-permute-done((bf16[2,128,128]{2,1,0:T(8,128)(2,1)}, bf16[2,128,128]{2,1,0:T(8,128)(2,1)S(1)}, u32[]{:S(2)}, u32[]{:S(2)}) %collective-permute-start) | collective-permute-done | bytes 65568 | tf_op jit(solution)/shard_map/ppermute | solution.py:16
  7.4 5.4 %collective-permute-start.1 = (bf16[2,256,128]{2,1,0:T(8,128)(2,1)S(1)}, bf16[2,256,128]{2,1,0:T(8,128)(2,1)S(1)}, u32[]{:S(2)}, u32[]{:S(2)}) collective-permute-start(bf16[2,256,128]{2,1,0:T(8,128)(2,1)S(1)} %constant_dynamic-update-slice_fusion), channel_id=1, source_target_pairs={{1,0},{2,1},{3,2},{4,3},{5,4},{6,5},{7,6},{8,7},{9,8},{10,9},{11,1... | collective-permute-start | bytes 393224 | tf_op jit(solution)/shard_map/ppermute | solution.py:16
  12.7 1.9 %collective-permute-done.1 = bf16[2,256,128]{2,1,0:T(8,128)(2,1)S(1)} collective-permute-done((bf16[2,256,128]{2,1,0:T(8,128)(2,1)S(1)}, bf16[2,256,128]{2,1,0:T(8,128)(2,1)S(1)}, u32[]{:S(2)}, u32[]{:S(2)}) %collective-permute-start.1) | collective-permute-done | bytes 131104 | tf_op jit(solution)/shard_map/ppermute | solution.py:16
  15.4 83.8 %while.18 = (s32[]{:T(128)}, f32[2,256,256]{2,1,0:T(8,128)S(1)}, f32[2,4,128,128]{3,2,1,0:T(8,128)S(1)}, s32[1,2,4]{2,1,0:T(2,128)S(1)}, s32[]{:T(128)}, /*index...) while((s32[]{:T(128)}, f32[2,256,256]{2,1,0:T(8,128)S(1)}, ...), condition=%wide.region_4.5_spmd.clone.clone, body=%wide.region_0.4_spmd.clone.clone.sunk | while | flops 1617985536 | bytes 16646421 | solution.py:135
  20.2 0.8 fusion.235
  20.9 0.8 fusion.236
  21.7 0.8 fusion.232
  22.5 0.8 fusion.233
  26.2 0.9 fusion.238
  27.8 0.7 fusion.243
  29.3 0.7 fusion.240
  32.2 0.8 add_bitcast_fusion.2
  34.0 2.2 %dynamic_update_slice.11 = f32[2,256,256]{2,1,0:T(8,128)S(1)} dynamic-update-slice(f32[2,256,256]{2,1,0:T(8,128)S(1)} %get-tuple-element.443, f32[2,128,128]{2,1,0:T(8,128)S(1)} %fusion.245, s32[]{:T(128)} %constant.67.clone.1..sunk, s32[]{:T(128)S(6)} %select_n.177, s32[]{:T(128)S(6)} %select_n.178) | dynamic-update-slice | bytes 262148 | tf_op jit(solution)/shard_map/while/body/eval_jaxpr/dynamic_update_slice | solution.py:129
  41.1 0.8 fusion.235
  41.8 0.8 fusion.236
  42.6 0.8 fusion.232
  43.4 0.8 fusion.233
  47.1 0.9 fusion.238
  48.7 0.7 fusion.243
  53.1 0.8 add_bitcast_fusion.2
  54.9 2.1 %dynamic_update_slice.11 = f32[2,256,256]{2,1,0:T(8,128)S(1)} dynamic-update-slice(f32[2,256,256]{2,1,0:T(8,128)S(1)} %get-tuple-element.443, f32[2,128,128]{2,1,0:T(8,128)S(1)} %fusion.245, s32[]{:T(128)} %constant.67.clone.1..sunk, s32[]{:T(128)S(6)} %select_n.177, s32[]{:T(128)S(6)} %select_n.178) | dynamic-update-slice | bytes 262148 | tf_op jit(solution)/shard_map/while/body/eval_jaxpr/dynamic_update_slice | solution.py:129
  61.8 0.8 fusion.235
  62.6 0.8 fusion.236
  63.4 0.8 fusion.232
  64.2 0.8 fusion.233
  67.8 0.9 fusion.238
  73.9 0.8 add_bitcast_fusion.2
  75.7 2.3 %dynamic_update_slice.11 = f32[2,256,256]{2,1,0:T(8,128)S(1)} dynamic-update-slice(f32[2,256,256]{2,1,0:T(8,128)S(1)} %get-tuple-element.443, f32[2,128,128]{2,1,0:T(8,128)S(1)} %fusion.245, s32[]{:T(128)} %constant.67.clone.1..sunk, s32[]{:T(128)S(6)} %select_n.177, s32[]{:T(128)S(6)} %select_n.178) | dynamic-update-slice | bytes 262148 | tf_op jit(solution)/shard_map/while/body/eval_jaxpr/dynamic_update_slice | solution.py:129
  82.8 0.8 fusion.235
  83.6 0.8 fusion.236
  84.3 0.8 fusion.232
  85.1 0.8 fusion.233
  88.8 0.9 fusion.238
  90.4 0.7 fusion.243
  94.9 0.8 add_bitcast_fusion.2
  96.6 2.3 %dynamic_update_slice.11 = f32[2,256,256]{2,1,0:T(8,128)S(1)} dynamic-update-slice(f32[2,256,256]{2,1,0:T(8,128)S(1)} %get-tuple-element.443, f32[2,128,128]{2,1,0:T(8,128)S(1)} %fusion.245, s32[]{:T(128)} %constant.67.clone.1..sunk, s32[]{:T(128)S(6)} %select_n.177, s32[]{:T(128)S(6)} %select_n.178) | dynamic-update-slice | bytes 262148 | tf_op jit(solution)/shard_map/while/body/eval_jaxpr/dynamic_update_slice | solution.py:129
  99.4 23.1 %all_to_all.20 = f32[32,16,2,128]{3,2,1,0:T(2,128)S(1)} all-to-all(f32[32,16,2,128]{3,2,1,0:T(2,128)S(1)} %copy.91), channel_id=1, replica_groups=mesh['region_0'=8,'region_1'=2,'pos_0'=4,'pos_1'=8] {'pos_0','pos_1'}, dimensions={0} | all-to-all | bytes 1048576 | tf_op jit(solution)/shard_map/all_to_all | solution.py:51
  122.7 18.8 %all_to_all.21 = f32[16,2,128]{2,1,0:T(2,128)S(1)} all-to-all(f32[16,2,128]{2,1,0:T(2,128)S(1)} %reduce_sum.60), channel_id=1, replica_groups=mesh['region_0'=8,'region_1'=2,'pos_0'=4,'pos_1'=8] {'region_0','region_1'}, dimensions={0} | all-to-all | bytes 32768 | tf_op jit(solution)/shard_map/all_to_all | solution.py:58
  141.6 10.2 %all_to_all.22 = f32[16,2,128]{2,1,0:T(2,128)S(1)} all-to-all(f32[16,2,128]{2,1,0:T(2,128)S(1)} %broadcast_in_dim.20), channel_id=1, replica_groups=mesh['region_0'=8,'region_1'=2,'pos_0'=4,'pos_1'=8] {'region_0','region_1'}, dimensions={0} | all-to-all | bytes 32768 | tf_op jit(solution)/shard_map/all_to_all | solution.py:28
  151.7 1.0 broadcast_in_dim.21
  152.8 6.8 %all-to-all-start.3 = ((f32[32,16,2,128]{3,2,1,0:T(2,128)}), f32[32,16,2,128]{3,2,1,0:T(2,128)S(1)}, u32[]{:S(2)}, u32[]{:S(2)}) async-start(f32[32,16,2,128]{3,2,1,0:T(2,128)} %broadcast_in_dim.21), calls=%async_computation.3 | async-start | bytes 1048576 | tf_op jit(solution)/shard_map/all_to_all | solution.py:28
  159.6 3.0 %collective-permute-start.2 = (f32[2,128,256]{2,1,0:T(8,128)S(1)}, f32[2,128,256]{2,1,0:T(8,128)S(1)}, u32[]{:S(2)}, u32[]{:S(2)}) collective-permute-start(f32[2,128,256]{2,1,0:T(8,128)S(1)} %slice.57), channel_id=1, source_target_pairs={{0,32},{32,64},{64,96},{96,128},{128,160},{160,192},{192,224},{224... | collective-permute-start | bytes 786440 | tf_op jit(solution)/shard_map/ppermute | solution.py:16
  162.6 3.3 %collective-permute-done.2 = f32[2,128,256]{2,1,0:T(8,128)S(1)} collective-permute-done((f32[2,128,256]{2,1,0:T(8,128)S(1)}, f32[2,128,256]{2,1,0:T(8,128)S(1)}, u32[]{:S(2)}, u32[]{:S(2)}) %collective-permute-start.2) | collective-permute-done | bytes 262176 | tf_op jit(solution)/shard_map/ppermute | solution.py:16
  165.9 3.1 %collective-permute-start.3 = (f32[2,128,128]{2,1,0:T(8,128)S(1)}, f32[2,128,128]{2,1,0:T(8,128)S(1)}, u32[]{:S(2)}, u32[]{:S(2)}) collective-permute-start(f32[2,128,128]{2,1,0:T(8,128)S(1)} %slice.69), channel_id=1, source_target_pairs={{0,1},{1,2},{2,3},{3,4},{4,5},{5,6},{6,7},{7,8},{8,9},{9,10},{10,1... | collective-permute-start | bytes 393224 | tf_op jit(solution)/shard_map/ppermute | solution.py:16
  169.0 8.5 %collective-permute-done.3 = f32[2,128,128]{2,1,0:T(8,128)S(1)} collective-permute-done((f32[2,128,128]{2,1,0:T(8,128)S(1)}, f32[2,128,128]{2,1,0:T(8,128)S(1)}, u32[]{:S(2)}, u32[]{:S(2)}) %collective-permute-start.3) | collective-permute-done | bytes 131104 | tf_op jit(solution)/shard_map/ppermute | solution.py:16
  178.6 1.1 copy.93
  (74 shorter events, 35.6 us)
Async XLA Ops:
  0.6 6.7 %collective-permute-start = (bf16[2,128,128]{2,1,0:T(8,128)(2,1)}, bf16[2,128,128]{2,1,0:T(8,128)(2,1)S(1)}, u32[]{:S(2)}, u32[]{:S(2)}) collective-permute-start(bf16[2,128,128]{2,1,0:T(8,128)(2,1)} %param.7), channel_id=1, source_target_pairs={{32,0},{64,32},{96,64},{128,96},{160,128},{192,160},{224,192},{256... | collective-permute-start | bytes 196616 | tf_op jit(solution)/shard_map/ppermute | solution.py:16
  7.4 7.3 %collective-permute-start.1 = (bf16[2,256,128]{2,1,0:T(8,128)(2,1)S(1)}, bf16[2,256,128]{2,1,0:T(8,128)(2,1)S(1)}, u32[]{:S(2)}, u32[]{:S(2)}) collective-permute-start(bf16[2,256,128]{2,1,0:T(8,128)(2,1)S(1)} %constant_dynamic-update-slice_fusion), channel_id=1, source_target_pairs={{1,0},{2,1},{3,2},{4,3},{5,4},{6,5},{7,6},{8,7},{9,8},{10,9},{11,1... | collective-permute-start | bytes 393224 | tf_op jit(solution)/shard_map/ppermute | solution.py:16
  12.7 2.0 %copy-start = (f32[2,4,128,128]{3,2,1,0:T(8,128)S(1)}, f32[2,4,128,128]{3,2,1,0:T(8,128)}, u32[]{:S(2)}) copy-start(f32[2,4,128,128]{3,2,1,0:T(8,128)} %param.8) | copy-start | bytes 1572868
  14.7 0.7 copy-start.1
  152.8 25.5 %all-to-all-start.3 = ((f32[32,16,2,128]{3,2,1,0:T(2,128)}), f32[32,16,2,128]{3,2,1,0:T(2,128)S(1)}, u32[]{:S(2)}, u32[]{:S(2)}) async-start(f32[32,16,2,128]{3,2,1,0:T(2,128)} %broadcast_in_dim.21), calls=%async_computation.3 | async-start | bytes 1048576 | tf_op jit(solution)/shard_map/all_to_all | solution.py:28
  159.6 6.3 %collective-permute-start.2 = (f32[2,128,256]{2,1,0:T(8,128)S(1)}, f32[2,128,256]{2,1,0:T(8,128)S(1)}, u32[]{:S(2)}, u32[]{:S(2)}) collective-permute-start(f32[2,128,256]{2,1,0:T(8,128)S(1)} %slice.57), channel_id=1, source_target_pairs={{0,32},{32,64},{64,96},{96,128},{128,160},{160,192},{192,224},{224... | collective-permute-start | bytes 786440 | tf_op jit(solution)/shard_map/ppermute | solution.py:16
  165.9 11.6 %collective-permute-start.3 = (f32[2,128,128]{2,1,0:T(8,128)S(1)}, f32[2,128,128]{2,1,0:T(8,128)S(1)}, u32[]{:S(2)}, u32[]{:S(2)}) collective-permute-start(f32[2,128,128]{2,1,0:T(8,128)S(1)} %slice.69), channel_id=1, source_target_pairs={{0,1},{1,2},{2,3},{3,4},{4,5},{5,6},{6,7},{7,8},{8,9},{9,10},{10,1... | collective-permute-start | bytes 393224 | tf_op jit(solution)/shard_map/ppermute | solution.py:16
where the time goes:
time: 181 us; the launch traced here: 180 us
  blocking collectives  52.1 us (29%)
  matrix products  47.6 us (26%)
  starting transfers between devices  20.8 us (11%)
  loops' own time  19.5 us (11%)
  waiting for transfers between devices  17 us (9%)
  local copies, waits for them, and re-layouts  16.1 us (9%)
  other arithmetic  5.82 us (3%)
    all_to_all x1, blocking collectives, sum_at_owner(): parts = lax.all_to_all(cut_along(shard, dim, count), axis, 0, 0, tiled=True)  23.1 us
    another operation x1, loops' own time, on_device(): grad_field, probe_sum = lax.fori_loop(0, slot_total, visit, start)  19.5 us
    all_to_all x1, blocking collectives, sum_in_two_steps(): return jnp.sum(lax.all_to_all(own, far, 0, 0, tiled=True), axis=0)  18.8 us
    ppermute x4, waiting for transfers between devices, passed_along(): return lax.ppermute(block, axis, route)  17 us
    ppermute x4, starting transfers between devices, passed_along(): return lax.ppermute(block, axis, route)  14.1 us
    all_to_all x1, blocking collectives, copy_for_each(): return lax.all_to_all(copies, axis, split_axis=0, concat_axis=0, tiled=True)  10.2 us
    dynamic_update_slice x4, local copies, waits for them, and re-layouts, visit(): lax.dynamic_update_slice(grad_field, current + weight * obj_term, (zero_i...  9.03 us
    all_to_all x1, starting transfers between devices, copy_for_each(): return lax.all_to_all(copies, axis, split_axis=0, concat_axis=0, tiled=True)  6.76 us
  transfers between devices with their start and end apart: 5, of which 4 were waited for; matrix products, arithmetic and copies ran while one was open for 1% of the time, Pallas kernels for 0%

commit v1 on v0

v1 whole, which is shorter than its diff:
```python
import functools
import math

import jax
import jax.numpy as jnp
import numpy as np
from jax import lax
from jax.experimental import pallas as pl
from jax.experimental.pallas import tpu as pltpu
from jax.sharding import PartitionSpec as P

MESH = pl.DeviceIdType.MESH
F32 = jnp.float32
BF16 = jnp.bfloat16
CHUNKS = 2


def dft_parts(order):
    index = np.arange(order)
    angle = (index[:, None] * index[None, :] % order) * (2.0 * math.pi / order)
    cos, sin = np.cos(angle) / math.sqrt(order), np.sin(angle) / math.sqrt(order)
    right = np.block([[cos, -sin], [sin, cos]]).astype(np.float32)
    parts = []
    for table in (right, right.T):
        high = table.astype(jnp.bfloat16)
        low = (table - high.astype(np.float32)).astype(jnp.bfloat16)
        parts.append(np.stack([high, low]))
    return np.stack(parts)


def split(value):
    high = value.astype(BF16)
    return high, (value - high.astype(F32)).astype(BF16)


def dot(a, b):
    return jnp.dot(a, b, preferred_element_type=F32)


def on_left(table, value):
    high, low = value
    return dot(
        jnp.concatenate([table[0], table[0], table[1]], axis=1),
        jnp.concatenate([high, low, high], axis=0),
    )


def on_right(value, table):
    high, low = value
    return dot(
        jnp.concatenate([high, low, high], axis=1),
        jnp.concatenate([table[0], table[0], table[1]], axis=0),
    )


def one_hot(shape, dim, shift, limit=None):
    along = lax.broadcasted_iota(jnp.int32, shape, dim)
    other = lax.broadcasted_iota(jnp.int32, shape, 1 - dim)
    hit = along == other + shift
    if limit is not None:
        hit = jnp.logical_and(hit, along < limit)
    return jnp.where(hit, 1.0, 0.0).astype(BF16)


def kernel(
    sizes, scale, tile, probe_h, amp_h, offsets, counts, tables_h, obj_out, probe_out,
    window, probe, amp, tables, crops, res_high, res_low, obj_terms, grads, terms, own, from_core, by_x, from_x, by_y,
    from_y, by_z, from_grad, load_sem, halo_send, halo_recv, grad_send, grad_recv, core_send, core_recv,
    x_send, x_recv, y_send, y_recv, z_send, z_recv, gy_send, gy_recv, gx_send, gx_recv, gc_send, gc_recv,
):
    nx, ny, nz, slots, modes, edge = sizes
    region, pos = lax.axis_index("region"), lax.axis_index("pos")
    n_region, n_pos = 2 * nz, nx * ny
    z, core = region // 2, lax.rem(region, 2)
    x, y = pos // ny, lax.rem(pos, ny)
    up, down = lax.rem(region + n_region - 1, n_region), lax.rem(region + 1, n_region)
    left, right = lax.rem(pos + n_pos - 1, n_pos), lax.rem(pos + 1, n_pos)
    sibling = (region + 1 - 2 * core, pos)

    def at_x(step):
        return (region, lax.rem(x + step, nx) * ny + y)

    def at_y(step):
        return (region, x * ny + lax.rem(y + step, ny))

    def at_z(step):
        return (lax.rem(z + step, nz) * 2 + core, pos)

    partners = [(up, left), (down, right), (up, pos), (down, pos), (region, left), (region, right), sibling]
    partners += [at_z(s) for s in range(1, nz)] + [at_y(s) for s in range(1, ny)] + [at_x(s) for s in range(1, nx)]
    barrier = pltpu.get_barrier_semaphore()
    for partner in partners:
        pl.semaphore_signal(barrier, inc=1, device_id=partner, device_id_type=MESH)

    loads = [
        pltpu.make_async_copy(tile, window.at[:, 0:edge, 0:edge], load_sem.at[0]),
        pltpu.make_async_copy(tables_h, tables, load_sem.at[1]),
        pltpu.make_async_copy(probe_h, probe, load_sem.at[2]),
        pltpu.make_async_copy(amp_h, amp, load_sem.at[3]),
    ]
    for load in loads:
        load.start()
    pl.semaphore_wait(barrier, len(partners))

    def send(src, dst, send_sem, recv_sem, device):
        copy = pltpu.make_async_remote_copy(
            src_ref=src, dst_ref=dst, send_sem=send_sem, recv_sem=recv_sem, device_id=device, device_id_type=MESH
        )
        copy.start()
        return copy

    second = slice(edge, 2 * edge)
    first = slice(0, edge)
    halo = [
        send(tile, window.at[:, second, second], halo_send.at[0], halo_recv.at[0], (up, left)),
        send(tile, window.at[:, second, first], halo_send.at[1], halo_recv.at[1], (up, pos)),
        send(tile, window.at[:, first, second], halo_send.at[2], halo_recv.at[2], (region, left)),
    ]
    for load in loads:
        load.wait()
    for copy in halo:
        copy.wait()

    row_limit = jnp.where(region < n_region - 1, 2 * edge, edge)
    col_limit = jnp.where(pos < n_pos - 1, 2 * edge, edge)
    live = counts[0, 0]

    def forward(slot, carry):
        row0, col0 = offsets[0, 0, slot], offsets[0, 1, slot]
        rows = one_hot((edge, 2 * edge), 1, row0, row_limit)
        cols = one_hot((2 * edge, edge), 0, col0, col_limit)
        lines = dot(rows, jnp.concatenate([window[0], window[1]], axis=1)).astype(BF16)
        crop = dot(jnp.concatenate([lines[:, : 2 * edge], lines[:, 2 * edge :]], axis=0), cols)
        crop_r, crop_i = crop[:edge], crop[edge:]
        crops[slot, 0], crops[slot, 1] = crop_r, crop_i
        exits = []
        for m in range(modes):
            probe_r, probe_i = probe[0, m], probe[1, m]
            exits.append(
                jnp.concatenate([probe_r * crop_r - probe_i * crop_i, probe_r * crop_i + probe_i * crop_r], axis=1)
            )
        half = on_right(split(jnp.concatenate(exits, axis=0)), tables.at[0])
        turned = jnp.concatenate(
            [
                jnp.concatenate([half[m * edge : (m + 1) * edge, :edge], half[m * edge : (m + 1) * edge, edge:]], axis=0)
                for m in range(modes)
            ],
            axis=1,
        )
        far = on_left(tables.at[1], split(turned))
        intensity = jnp.zeros((edge, edge), F32)
        for m in range(modes):
            part = far[:, m * edge : (m + 1) * edge]
            intensity += part[:edge] * part[:edge] + part[edge:] * part[edge:]
        factor = 1.0 - amp[0, slot] / jnp.sqrt(intensity + 1.0)
        factor = jnp.where(slot < live, factor, 0.0)
        for m in range(modes):
            lanes = slice(m * edge, (m + 1) * edge)
            high, low = split(far[:, lanes] * jnp.concatenate([factor, factor], axis=0))
            res_high[slot, :, lanes] = high
            res_low[slot, :, lanes] = low
        return carry

    lax.fori_loop(0, slots, forward, 0)

    per = modes // CHUNKS

    def backward_of(chunk):
        def backward(slot, carry):
            lanes = slice(chunk * per * edge, (chunk + 1) * per * edge)
            half = on_left(tables.at[0], (res_high[slot, :, lanes], res_low[slot, :, lanes]))
            turned = jnp.concatenate(
                [
                    jnp.concatenate(
                        [half[:edge, m * edge : (m + 1) * edge], half[edge:, m * edge : (m + 1) * edge]], axis=1
                    )
                    for m in range(per)
                ],
                axis=0,
            )
            back = on_right(split(turned), tables.at[1])
            crop_r, crop_i = crops[slot, 0], crops[slot, 1]
            obj_r, obj_i = 0.0, 0.0
            for m in range(per):
                back_r, back_i = back[m * edge : (m + 1) * edge, :edge], back[m * edge : (m + 1) * edge, edge:]
                probe_r, probe_i = probe[0, chunk * per + m], probe[1, chunk * per + m]
                obj_r += probe_r * back_r + probe_i * back_i
                obj_i += probe_r * back_i - probe_i * back_r
                lines = slice(m * edge, (m + 1) * edge)
                terms[0, chunk, lines] += crop_r * back_r + crop_i * back_i
                terms[1, chunk, lines] += crop_r * back_i - crop_i * back_r
            if chunk == 0:
                obj_terms[slot, 0], obj_terms[slot, 1] = obj_r, obj_i
            else:
                obj_terms[slot, 0] += obj_r
                obj_terms[slot, 1] += obj_i
            return carry

        terms[:, chunk] = jnp.zeros((2, per * edge, edge), F32)
        lax.fori_loop(0, slots, backward, 0)

    def place(slot, carry):
        row0, col0 = offsets[0, 0, slot], offsets[0, 1, slot]
        cols = one_hot((edge, 2 * edge), 1, col0)
        rows = one_hot((2 * edge, edge), 0, row0)
        high_r, low_r = split(obj_terms[slot, 0])
        high_i, low_i = split(obj_terms[slot, 1])
        wide = dot(jnp.concatenate([high_r, high_i, low_r, low_i], axis=0), cols)
        wide = wide[: 2 * edge] + wide[2 * edge :]
        high, low = split(jnp.concatenate([wide[:edge], wide[edge:]], axis=1))
        field = dot(jnp.concatenate([rows, rows], axis=1), jnp.concatenate([high, low], axis=0))
        grads[0] += field[:, : 2 * edge]
        grads[1] += field[:, 2 * edge :]
        return carry

    pending = []
    chunk_rows = per * edge
    x_rows, y_rows = chunk_rows // nx, chunk_rows // nx // ny

    def core_scatter(q):
        copy = send(terms.at[1 - core, q], from_core.at[q], core_send.at[q], core_recv.at[q], sibling)
        pending.append(copy)
        return [copy]

    def x_scatter(q, arrived):
        for copy in arrived:
            copy.wait_recv()
        own[q] = terms[core, q] + from_core[q]
        copies = []
        for s in sorted(range(1, nx), key=lambda s: -min(s, nx - s)):
            rows = pl.ds(pl.multiple_of(lax.rem(x + s, nx) * x_rows, x_rows), x_rows)
            copies.append(
                send(own.at[q, rows], from_x.at[q, s - 1], x_send.at[q, s - 1], x_recv.at[q, s - 1], at_x(s))
            )
        pending.extend(copies)
        return copies

    def y_scatter(q, arrived):
        for copy in arrived:
            copy.wait_recv()
        total = own[q, pl.ds(pl.multiple_of(x * x_rows, x_rows), x_rows)]
        for s in range(1, nx):
            total += from_x[q, s - 1]
        by_x[q] = total
        copies = []
        for s in sorted(range(1, ny), key=lambda s: -min(s, ny - s)):
            rows = pl.ds(pl.multiple_of(lax.rem(y + s, ny) * y_rows, y_rows), y_rows)
            copies.append(
                send(by_x.at[q, rows], from_y.at[q, s - 1], y_send.at[q, s - 1], y_recv.at[q, s - 1], at_y(s))
            )
        pending.extend(copies)
        return copies

    def z_gather(q, arrived):
        for copy in arrived:
            copy.wait_recv()
        total = by_x[q, pl.ds(pl.multiple_of(y * y_rows, y_rows), y_rows)]
        for s in range(1, ny):
            total += from_y[q, s - 1]
        by_z[q, z] = total
        copies = []
        for s in sorted(range(1, nz), key=lambda s: -min(s, nz - s)):
            copies.append(
                send(by_z.at[q, z], by_z.at[q, z], z_send.at[q, s - 1], z_recv.at[q, s - 1], at_z(s))
            )
        pending.extend(copies)
        return copies

    def y_gather(q, arrived):
        for copy in arrived:
            copy.wait_recv()
        total = by_z[q, 0]
        for s in range(1, nz):
            total += by_z[q, s]
        mine = probe_out.at[core, q, pl.ds(pl.multiple_of(x * x_rows + y * y_rows, y_rows), y_rows)]
        mine[...] = total * scale
        copies = []
        for s in sorted(range(1, ny), key=lambda s: -min(s, ny - s)):
            copies.append(send(mine, mine, gy_send.at[q, s - 1], gy_recv.at[q, s - 1], at_y(s)))
        pending.extend(copies)
        return copies

    def x_gather(q, arrived):
        for copy in arrived:
            copy.wait_recv()
        mine = probe_out.at[core, q, pl.ds(pl.multiple_of(x * x_rows, x_rows), x_rows)]
        copies = []
        for s in sorted(range(1, nx), key=lambda s: -min(s, nx - s)):
            copies.append(send(mine, mine, gx_send.at[q, s - 1], gx_recv.at[q, s - 1], at_x(s)))
        pending.extend(copies)
        return copies

    def core_gather(q, arrived):
        for copy in arrived:
            copy.wait_recv()
        mine = probe_out.at[core, q]
        copy = send(mine, mine, gc_send.at[q], gc_recv.at[q], sibling)
        pending.append(copy)
        return [copy]

    backward_of(0)
    state = [core_scatter(0), None]
    backward_of(1)
    state[1] = core_scatter(1)
    state[0] = x_scatter(0, state[0])
    grads[...] = jnp.zeros_like(grads)
    lax.fori_loop(0, slots, place, 0)
    state[1] = x_scatter(1, state[1])
    state[0] = y_scatter(0, state[0])
    grad_copies = [
        send(grads.at[:, second, second], from_grad.at[0], grad_send.at[0], grad_recv.at[0], (down, right)),
        send(grads.at[:, second, first], from_grad.at[1], grad_send.at[1], grad_recv.at[1], (down, pos)),
        send(grads.at[:, first, second], from_grad.at[2], grad_send.at[2], grad_recv.at[2], (region, right)),
    ]
    for phase in (y_scatter, z_gather, y_gather, x_gather, core_gather):
        if phase is not y_scatter:
            state[0] = phase(0, state[0])
        state[1] = phase(1, state[1])
        if phase is z_gather:
            for copy in grad_copies:
                copy.wait()
            total = grads[:, first, first]
            total += jnp.where(pos > 0, from_grad[2], 0.0)
            total += jnp.where(region > 0, from_grad[1], 0.0)
            total += jnp.where(jnp.logical_and(region > 0, pos > 0), from_grad[0], 0.0)
            obj_out[...] = total
    for copies in state:
        for copy in copies:
            copy.wait_recv()
    for copy in pending:
        copy.wait_send()


def solution(mesh):
    n_region, n_pos = mesh.shape["region"], mesh.shape["pos"]
    nz = n_region // 2
    nx = 4 if n_pos == 32 else 2
    ny = n_pos // nx

    def on_device(object_tiles, probe, amplitudes, offsets, counts):
        modes, edge = probe.shape[1], probe.shape[2]
        slots = amplitudes.shape[1]
        rows = modes // CHUNKS * edge
        x_rows, y_rows = rows // nx, rows // nx // ny
        scale = 1.0 / math.sqrt(n_region * n_pos * slots)
        dma = pltpu.SemaphoreType.DMA
        any_space = pl.BlockSpec(memory_space=pl.ANY)
        vmem_space = pl.BlockSpec(memory_space=pltpu.VMEM)
        smem_space = pl.BlockSpec(memory_space=pltpu.SMEM)
        sizes = (nx, ny, nz, slots, modes, edge)
        phase_sems = []
        for count in (0, nx - 1, ny - 1, nz - 1, ny - 1, nx - 1, 0):
            shape = (CHUNKS, count) if count else (CHUNKS,)
            phase_sems += [dma(shape), dma(shape)]
        obj_grad, probe_grad = pl.pallas_call(
            functools.partial(kernel, sizes, scale),
            out_shape=(
                jax.ShapeDtypeStruct((2, edge, edge), F32),
                jax.ShapeDtypeStruct((2, CHUNKS, rows, edge), F32),
            ),
            in_specs=[vmem_space, any_space, any_space, smem_space, smem_space, any_space],
            out_specs=(vmem_space, vmem_space),
            scratch_shapes=[
                pltpu.VMEM((2, 2 * edge, 2 * edge), BF16),
                pltpu.VMEM((2, modes, edge, edge), F32),
                pltpu.VMEM((1, slots, edge, edge), F32),
                pltpu.VMEM((2, 2, 2 * edge, 2 * edge), BF16),
                pltpu.VMEM((slots, 2, edge, edge), F32),
                pltpu.VMEM((slots, 2 * edge, modes * edge), BF16),
                pltpu.VMEM((slots, 2 * edge, modes * edge), BF16),
                pltpu.VMEM((slots, 2, edge, edge), F32),
                pltpu.VMEM((2, 2 * edge, 2 * edge), F32),
                pltpu.VMEM((2, CHUNKS, rows, edge), F32),
                pltpu.VMEM((CHUNKS, rows, edge), F32),
                pltpu.VMEM((CHUNKS, rows, edge), F32),
                pltpu.VMEM((CHUNKS, x_rows, edge), F32),
                pltpu.VMEM((CHUNKS, nx - 1, x_rows, edge), F32),
                pltpu.VMEM((CHUNKS, y_rows, edge), F32),
                pltpu.VMEM((CHUNKS, ny - 1, y_rows, edge), F32),
                pltpu.VMEM((CHUNKS, nz, y_rows, edge), F32),
                pltpu.VMEM((3, 2, edge, edge), F32),
                dma((4,)), dma((3,)), dma((3,)), dma((3,)), dma((3,)),
                *phase_sems,
            ],
            compiler_params=pltpu.CompilerParams(collective_id=0, has_side_effects=True),
        )(object_tiles, probe, amplitudes, offsets, counts, jnp.asarray(dft_parts(edge)))
        return obj_grad, probe_grad.reshape(2, modes, edge, edge)

    return jax.shard_map(
        on_device,
        mesh=mesh,
        in_specs=(
            P(None, "region", "pos"),
            P(),
            P("region", "pos", None, None),
            P("region", None, "pos"),
            P("region", "pos"),
        ),
        out_specs=(P(None, "region", "pos"), P()),
        check_vma=False,
    )
```

time: 181 us -> 66.4 us (0.37)
  the two profiles are of different devices: /device:TPU:7 before, /device:TPU:1 now
where the time goes in v1:
time: 66.4 us; the launch traced here: 66.1 us
  Pallas kernels  61.4 us (92%)
  local copies, waits for them, and re-layouts  3.44 us (5%)
  between operations  1.29 us (2%)
    pallas_call x1, Pallas kernels, on_device(): pl.pallas_call(functools.partial(kernel, sizes, scale), out_shape=(jax.Sh...  61.4 us
    unnamed x2, local copies, waits for them, and re-layouts  3.44 us

profile of v1, /device:TPU:1, one launch (start us, length us, event | category | flops | bytes accessed | tf_op | source)
XLA Modules:
  0.0 66.1 jit_solution(15860468301222195299)
XLA Ops:
  1.3 61.4 %shard_map.77 = (f32[2,128,128]{2,1,0:T(8,128)}, f32[2,2,256,128]{3,2,1,0:T(8,128)}) custom-call(bf16[2,128,128]{2,1,0:T(8,128)(2,1)} %tile.1, f32[2,4,128,128]{3,2,1,0:T(8,128)} %probe_h.1, f32[1,4,128,128]{3,2,1,0:T(8,128)} %amp_h.1, s32[1,2,4]{2,1,0:T(2,128)} %offsets.1, s32[1,1]{1,0:T(1,128)S(6)} %copy.10.counts, ...), custom_call_target="tpu_custom_call" | custom-call | tf_op jit(solution)/shard_map/pallas_call | solution.py:355
  62.7 1.6 %copy.11 = f32[2,128,128]{2,1,0:T(8,128)} copy(f32[2,128,128]{2,1,0:T(8,128)} %get-tuple-element.8) | data formatting | bytes 262144
  64.3 1.9 %copy.12 = f32[2,4,128,128]{3,2,1,0:T(8,128)} copy(f32[2,4,128,128]{3,2,1,0:T(8,128)} %bitcast.1) | data formatting | bytes 1048576

commit v2 on v1

v2 whole, which is shorter than its diff:
```python
import functools
import math

import jax
import jax.numpy as jnp
import numpy as np
from jax import lax
from jax.experimental import pallas as pl
from jax.experimental.pallas import tpu as pltpu
from jax.sharding import PartitionSpec as P

MESH = pl.DeviceIdType.MESH
F32 = jnp.float32
BF16 = jnp.bfloat16
CHUNKS = 2
GROUP = 2
UNROLL = 1


def dft_parts(order):
    index = np.arange(order)
    angle = (index[:, None] * index[None, :] % order) * (2.0 * math.pi / order)
    cos, sin = np.cos(angle) / math.sqrt(order), np.sin(angle) / math.sqrt(order)
    right = np.block([[cos, -sin], [sin, cos]]).astype(np.float32)
    parts = []
    for table in (right, right.T):
        high = table.astype(jnp.bfloat16)
        low = (table - high.astype(np.float32)).astype(jnp.bfloat16)
        parts.append(np.stack([high, low]))
    return np.stack(parts)


def split(value):
    high = value.astype(BF16)
    return high, (value - high.astype(F32)).astype(BF16)


def dot(a, b):
    return jnp.dot(a, b, preferred_element_type=F32)


def on_left(table, value):
    high, low = value
    return dot(
        jnp.concatenate([table[0], table[0], table[1]], axis=1),
        jnp.concatenate([high, low, high], axis=0),
    )


def on_right(value, table):
    high, low = value
    return dot(
        jnp.concatenate([high, low, high], axis=1),
        jnp.concatenate([table[0], table[0], table[1]], axis=0),
    )


def one_hot(shape, dim, shift, limit=None):
    along = lax.broadcasted_iota(jnp.int32, shape, dim)
    other = lax.broadcasted_iota(jnp.int32, shape, 1 - dim)
    hit = along == other + shift
    if limit is not None:
        hit = jnp.logical_and(hit, along < limit)
    return jnp.where(hit, 1.0, 0.0).astype(BF16)


def by_distance(count):
    return sorted(range(1, count), key=lambda step: -min(step, count - step))


def kernel(
    sizes, scale, tile, probe_h, amp_h, offsets_h, counts_h, tables_h, obj_out, probe_out,
    offsets, counts, window, probe, amp, tables, crops, res_high, res_low, backs, grads, terms, own, from_core, by_x,
    from_x, from_y, by_z, from_grad, load_sem, halo_send, halo_recv, grad_send, grad_recv, core_send, core_recv,
    x_send, x_recv, y_send, y_recv, z_send, z_recv, gy_send, gy_recv, gx_send, gx_recv, gc_send, gc_recv,
):
    nx, ny, nz, slots, modes, edge = sizes
    region, pos = lax.axis_index("region"), lax.axis_index("pos")
    n_region, n_pos = 2 * nz, nx * ny
    z, core = region // 2, lax.rem(region, 2)
    x, y = pos // ny, lax.rem(pos, ny)
    up, down = lax.rem(region + n_region - 1, n_region), lax.rem(region + 1, n_region)
    left, right = lax.rem(pos + n_pos - 1, n_pos), lax.rem(pos + 1, n_pos)
    sibling = (region + 1 - 2 * core, pos)

    def at_x(step):
        return (region, lax.rem(x + step, nx) * ny + y)

    def at_y(step):
        return (region, x * ny + lax.rem(y + step, ny))

    def at_z(step):
        return (lax.rem(z + step, nz) * 2 + core, pos)

    partners = [(down, right), (down, pos), (region, right), (up, left), (up, pos), (region, left), sibling]
    partners += [at_z(s) for s in by_distance(nz)] + [at_y(s) for s in by_distance(ny)]
    partners += [at_x(s) for s in by_distance(nx)]
    barrier = pltpu.get_barrier_semaphore()
    for partner in partners:
        pl.semaphore_signal(barrier, inc=1, device_id=partner, device_id_type=MESH)

    first, second = slice(0, edge), slice(edge, 2 * edge)
    loads = [
        pltpu.make_async_copy(offsets_h, offsets, load_sem.at[0]),
        pltpu.make_async_copy(counts_h, counts, load_sem.at[1]),
        pltpu.make_async_copy(tile, window.at[:, first, first], load_sem.at[2]),
        pltpu.make_async_copy(probe_h, probe, load_sem.at[3]),
        pltpu.make_async_copy(tables_h, tables, load_sem.at[4]),
        pltpu.make_async_copy(amp_h, amp, load_sem.at[5]),
    ]
    for load in loads:
        load.start()
    pl.semaphore_wait(barrier, len(partners))

    def send(src, dst, send_sem, recv_sem, device):
        copy = pltpu.make_async_remote_copy(
            src_ref=src, dst_ref=dst, send_sem=send_sem, recv_sem=recv_sem, device_id=device, device_id_type=MESH
        )
        copy.start()
        return copy

    halo = [
        send(tile, window.at[:, second, second], halo_send.at[0], halo_recv.at[0], (up, left)),
        send(tile, window.at[:, first, second], halo_send.at[2], halo_recv.at[2], (region, left)),
        send(tile, window.at[:, second, first], halo_send.at[1], halo_recv.at[1], (up, pos)),
    ]
    for load in loads:
        load.wait()
    for copy in halo:
        copy.wait()

    row_limit = jnp.where(region < n_region - 1, 2 * edge, edge)
    col_limit = jnp.where(pos < n_pos - 1, 2 * edge, edge)
    live = counts[0, 0]

    def forward(slot, carry):
        row0, col0 = offsets[0, 0, slot], offsets[0, 1, slot]
        rows = one_hot((edge, 2 * edge), 1, row0, row_limit)
        cols = one_hot((2 * edge, edge), 0, col0, col_limit)
        lines = dot(rows, jnp.concatenate([window[0], window[1]], axis=1)).astype(BF16)
        crop = dot(jnp.concatenate([lines[:, : 2 * edge], lines[:, 2 * edge :]], axis=0), cols)
        crop_r, crop_i = crop[:edge], crop[edge:]
        crops[slot, 0], crops[slot, 1] = crop_r, crop_i
        intensity = jnp.zeros((edge, edge), F32)
        fars = []
        for m in range(0, modes, GROUP):
            exits = []
            for n in range(m, m + GROUP):
                probe_r, probe_i = probe[0, n], probe[1, n]
                exits.append(
                    jnp.concatenate([probe_r * crop_r - probe_i * crop_i, probe_r * crop_i + probe_i * crop_r], axis=1)
                )
            half = on_right(split(jnp.concatenate(exits, axis=0)), tables.at[0])
            blocks = [half[n * edge : (n + 1) * edge] for n in range(GROUP)]
            turned = jnp.concatenate(
                [jnp.concatenate([block[:, :edge], block[:, edge:]], axis=0) for block in blocks], axis=1
            )
            far = on_left(tables.at[1], split(turned))
            for n in range(GROUP):
                part = far[:, n * edge : (n + 1) * edge]
                intensity += part[:edge] * part[:edge] + part[edge:] * part[edge:]
                fars.append(part)
        factor = 1.0 - amp[0, slot] / jnp.sqrt(intensity + 1.0)
        factor = jnp.where(slot < live, factor, 0.0)
        factor = jnp.concatenate([factor, factor], axis=0)
        for m in range(modes):
            high, low = split(fars[m] * factor)
            res_high[slot, m], res_low[slot, m] = high, low
        return carry

    lax.fori_loop(0, slots, forward, 0, unroll=UNROLL)

    per = modes // CHUNKS

    def backward_of(chunk):
        def backward(slot, carry):
            picks = range(chunk * per, (chunk + 1) * per)
            high = jnp.concatenate([res_high[slot, m] for m in picks], axis=1)
            low = jnp.concatenate([res_low[slot, m] for m in picks], axis=1)
            half = on_left(tables.at[0], (high, low))
            blocks = [half[:, n * edge : (n + 1) * edge] for n in range(per)]
            turned = jnp.concatenate(
                [jnp.concatenate([block[:edge], block[edge:]], axis=1) for block in blocks], axis=0
            )
            back = on_right(split(turned), tables.at[1])
            backs[slot, chunk] = back
            crop_r, crop_i = crops[slot, 0], crops[slot, 1]
            for n in range(per):
                lines = slice(n * edge, (n + 1) * edge)
                back_r, back_i = back[lines, :edge], back[lines, edge:]
                term_r = crop_r * back_r + crop_i * back_i
                term_i = crop_r * back_i - crop_i * back_r
                terms[0, chunk, lines] += term_r
                terms[1, chunk, lines] += term_i
            return carry

        return backward

    def place(slot):
        row0, col0 = offsets[0, 0, slot], offsets[0, 1, slot]
        cols = one_hot((edge, 2 * edge), 1, col0)
        rows = one_hot((2 * edge, edge), 0, row0)
        obj_r, obj_i = 0.0, 0.0
        for m in range(modes):
            lines = slice(m % per * edge, (m % per + 1) * edge)
            back_r, back_i = backs[slot, m // per, lines, first], backs[slot, m // per, lines, second]
            probe_r, probe_i = probe[0, m], probe[1, m]
            obj_r += probe_r * back_r + probe_i * back_i
            obj_i += probe_r * back_i - probe_i * back_r
        high_r, low_r = split(obj_r)
        high_i, low_i = split(obj_i)
        wide = dot(jnp.concatenate([high_r, high_i, low_r, low_i], axis=0), cols)
        wide = wide[: 2 * edge] + wide[2 * edge :]
        high, low = split(jnp.concatenate([wide[:edge], wide[edge:]], axis=1))
        field = dot(jnp.concatenate([rows, rows], axis=1), jnp.concatenate([high, low], axis=0))
        if slot == 0:
            grads[0], grads[1] = field[:, : 2 * edge], field[:, 2 * edge :]
        else:
            grads[0] += field[:, : 2 * edge]
            grads[1] += field[:, 2 * edge :]

    pending = []
    chunk_rows = per * edge
    x_rows, y_rows = chunk_rows // nx, chunk_rows // nx // ny

    def x_lines(step=0):
        return pl.ds(pl.multiple_of(lax.rem(x + step, nx) * x_rows, x_rows), x_rows)

    def y_lines(step=0):
        return pl.ds(pl.multiple_of(lax.rem(y + step, ny) * y_rows, y_rows), y_rows)

    def sent(copies):
        pending.extend(copies)
        return copies

    def core_scatter(q):
        return sent([send(terms.at[1 - core, q], from_core.at[q], core_send.at[q], core_recv.at[q], sibling)])

    def x_scatter(q, arrived):
        for copy in arrived:
            copy.wait_recv()
        own[q] = terms[core, q] + from_core[q]
        return sent(
            [
                send(own.at[q, x_lines(s)], from_x.at[q, s - 1], x_send.at[q, s - 1], x_recv.at[q, s - 1], at_x(s))
                for s in by_distance(nx)
            ]
        )

    def y_scatter(q, arrived):
        for copy in arrived:
            copy.wait_recv()
        total = own[q, x_lines()]
        for s in range(1, nx):
            total += from_x[q, s - 1]
        by_x[q] = total
        return sent(
            [
                send(by_x.at[q, y_lines(s)], from_y.at[q, s - 1], y_send.at[q, s - 1], y_recv.at[q, s - 1], at_y(s))
                for s in by_distance(ny)
            ]
        )

    def z_gather(q, arrived):
        for copy in arrived:
            copy.wait_recv()
        total = by_x[q, y_lines()]
        for s in range(1, ny):
            total += from_y[q, s - 1]
        by_z[q, z] = total
        return sent(
            [
                send(by_z.at[q, z], by_z.at[q, z], z_send.at[q, s - 1], z_recv.at[q, s - 1], at_z(s))
                for s in by_distance(nz)
            ]
        )

    def y_gather(q, arrived):
        for copy in arrived:
            copy.wait_recv()
        total = by_z[q, 0]
        for s in range(1, nz):
            total += by_z[q, s]
        mine = probe_out.at[core, q, pl.ds(pl.multiple_of(x * x_rows + y * y_rows, y_rows), y_rows)]
        mine[...] = total * scale
        return sent(
            [send(mine, mine, gy_send.at[q, s - 1], gy_recv.at[q, s - 1], at_y(s)) for s in by_distance(ny)]
        )

    def x_gather(q, arrived):
        for copy in arrived:
            copy.wait_recv()
        mine = probe_out.at[core, q, x_lines()]
        copies = sent([send(mine, mine, gx_send.at[q, s - 1], gx_recv.at[q, s - 1], at_x(s)) for s in by_distance(nx)])
        to_core = sent([send(mine, mine, gc_send.at[q, 0], gc_recv.at[q, 0], sibling)])
        return copies, to_core

    def core_gather(q, arrived):
        copies, to_core = arrived
        steps = by_distance(nx)
        for s, copy in sorted(zip(steps, copies), key=lambda pair: min(pair[0], nx - pair[0])):
            copy.wait_recv()
            piece = probe_out.at[core, q, x_lines(nx - s)]
            to_core += sent([send(piece, piece, gc_send.at[q, s], gc_recv.at[q, s], sibling)])
        return to_core

    terms[...] = jnp.zeros_like(terms)
    lax.fori_loop(0, slots, backward_of(0), 0, unroll=UNROLL)
    front = core_scatter(0)
    lax.fori_loop(0, slots // 2, backward_of(1), 0, unroll=UNROLL)
    front = x_scatter(0, front)
    lax.fori_loop(slots // 2, slots, backward_of(1), 0, unroll=UNROLL)
    back = core_scatter(1)
    place(0)
    back = x_scatter(1, back)
    front = y_scatter(0, front)
    for slot in range(1, max(2, slots // 2)):
        place(slot)
    back = y_scatter(1, back)
    front = z_gather(0, front)
    for slot in range(max(2, slots // 2), slots):
        place(slot)
    grad_copies = [
        send(grads.at[:, second, second], from_grad.at[0], grad_send.at[0], grad_recv.at[0], (down, right)),
        send(grads.at[:, first, second], from_grad.at[2], grad_send.at[2], grad_recv.at[2], (region, right)),
        send(grads.at[:, second, first], from_grad.at[1], grad_send.at[1], grad_recv.at[1], (down, pos)),
    ]
    back = z_gather(1, back)
    front = y_gather(0, front)
    back = y_gather(1, back)
    front = x_gather(0, front)
    for copy in grad_copies:
        copy.wait()
    total = grads[:, first, first]
    total += jnp.where(pos > 0, from_grad[2], 0.0)
    total += jnp.where(region > 0, from_grad[1], 0.0)
    total += jnp.where(jnp.logical_and(region > 0, pos > 0), from_grad[0], 0.0)
    obj_out[...] = total
    back = x_gather(1, back)
    front = core_gather(0, front)
    back = core_gather(1, back)
    for copy in front + back:
        copy.wait_recv()
    for copy in pending:
        copy.wait_send()


def finish(obj_in, probe_in, obj_out, probe_out, sems):
    copies = [
        pltpu.make_async_copy(probe_in, probe_out, sems.at[0]),
        pltpu.make_async_copy(obj_in, obj_out, sems.at[1]),
    ]
    for copy in copies:
        copy.start()
    for copy in copies:
        copy.wait()


def solution(mesh):
    n_region, n_pos = mesh.shape["region"], mesh.shape["pos"]
    nz = n_region // 2
    nx = 4 if n_pos == 32 else 2
    ny = n_pos // nx

    def on_device(object_tiles, probe, amplitudes, offsets, counts):
        modes, edge = probe.shape[1], probe.shape[2]
        slots = amplitudes.shape[1]
        rows = modes // CHUNKS * edge
        x_rows, y_rows = rows // nx, rows // nx // ny
        scale = 1.0 / math.sqrt(n_region * n_pos * slots)
        dma = pltpu.SemaphoreType.DMA
        any_space = pl.BlockSpec(memory_space=pl.ANY)
        vmem_space = pl.BlockSpec(memory_space=pltpu.VMEM)
        sizes = (nx, ny, nz, slots, modes, edge)
        phase_sems = []
        for count in (0, nx - 1, ny - 1, nz - 1, ny - 1, nx - 1, nx):
            shape = (CHUNKS, count) if count else (CHUNKS,)
            phase_sems += [dma(shape), dma(shape)]
        held = pl.pallas_call(
            functools.partial(kernel, sizes, scale),
            out_shape=(pltpu.VMEM((2, edge, edge), F32), pltpu.VMEM((2, CHUNKS, rows, edge), F32)),
            in_specs=[any_space] * 6,
            out_specs=(vmem_space, vmem_space),
            scratch_shapes=[
                pltpu.SMEM((1, 2, slots), jnp.int32),
                pltpu.SMEM((1, 1), jnp.int32),
                pltpu.VMEM((2, 2 * edge, 2 * edge), BF16),
                pltpu.VMEM((2, modes, edge, edge), F32),
                pltpu.VMEM((1, slots, edge, edge), F32),
                pltpu.VMEM((2, 2, 2 * edge, 2 * edge), BF16),
                pltpu.VMEM((slots, 2, edge, edge), F32),
                pltpu.VMEM((slots, modes, 2 * edge, edge), BF16),
                pltpu.VMEM((slots, modes, 2 * edge, edge), BF16),
                pltpu.VMEM((slots, CHUNKS, rows, 2 * edge), F32),
                pltpu.VMEM((2, 2 * edge, 2 * edge), F32),
                pltpu.VMEM((2, CHUNKS, rows, edge), F32),
                pltpu.VMEM((CHUNKS, rows, edge), F32),
                pltpu.VMEM((CHUNKS, rows, edge), F32),
                pltpu.VMEM((CHUNKS, x_rows, edge), F32),
                pltpu.VMEM((CHUNKS, nx - 1, x_rows, edge), F32),
                pltpu.VMEM((CHUNKS, ny - 1, y_rows, edge), F32),
                pltpu.VMEM((CHUNKS, nz, y_rows, edge), F32),
                pltpu.VMEM((3, 2, edge, edge), F32),
                dma((6,)), dma((3,)), dma((3,)), dma((3,)), dma((3,)),
                *phase_sems,
            ],
            compiler_params=pltpu.CompilerParams(collective_id=0, has_side_effects=True),
        )(object_tiles, probe, amplitudes, offsets, counts, jnp.asarray(dft_parts(edge)))
        obj_grad, probe_grad = pl.pallas_call(
            finish,
            out_shape=(
                jax.ShapeDtypeStruct((2, edge, edge), F32),
                jax.ShapeDtypeStruct((2, CHUNKS, rows, edge), F32),
            ),
            in_specs=[vmem_space] * 2,
            out_specs=(any_space, any_space),
            scratch_shapes=[dma((2,))],
        )(*[pltpu.with_memory_space_constraint(v, pltpu.VMEM) for v in held])
        return obj_grad, probe_grad.reshape(2, modes, edge, edge)

    return jax.shard_map(
        on_device,
        mesh=mesh,
        in_specs=(
            P(None, "region", "pos"),
            P(),
            P("region", "pos", None, None),
            P("region", None, "pos"),
            P("region", "pos"),
        ),
        out_specs=(P(None, "region", "pos"), P()),
        check_vma=False,
    )
```

time: 66.4 us -> 58 us (0.87)
  Pallas kernels: 61.4 us -> 56.6 us
  local copies, waits for them, and re-layouts: 3.44 us -> 0 us
    pallas_call x1 -> x2, Pallas kernels: 61.4 us -> 56.6 us  [the longest x1 55.7 us: on_device(): pl.pallas_call(functools.partial(kernel, sizes, scale), out_shape=(pltpu....]
    unnamed x2 -> x0, local copies, waits for them, and re-layouts: 3.44 us -> none
where the time goes in v2:
time: 58 us; the launch traced here: 57.9 us
  Pallas kernels  56.6 us (98%)
  between operations  1.29 us (2%)
    pallas_call x1, Pallas kernels, on_device(): pl.pallas_call(functools.partial(kernel, sizes, scale), out_shape=(pltpu....  55.7 us

profile of v2, /device:TPU:1, one launch (start us, length us, event | category | flops | bytes accessed | tf_op | source)
XLA Modules:
  0.0 57.9 jit_solution(13182126012407489741)
XLA Ops:
  1.3 55.7 %shard_map.77 = (f32[2,128,128]{2,1,0:T(8,128)S(1)}, f32[2,2,256,128]{3,2,1,0:T(8,128)S(1)}) custom-call(bf16[2,128,128]{2,1,0:T(8,128)(2,1)} %tile.1, f32[2,4,128,128]{3,2,1,0:T(8,128)} %probe_h.1, f32[1,4,128,128]{3,2,1,0:T(8,128)} %amp_h.1, s32[1,2,4]{2,1,0:T(2,128)} %offsets_h.1, s32[1,1]{1,0:T(1,128)S(6)} %copy.8.counts_h, ...), custom_call_target="tpu_custom_call" | custom-call | tf_op jit(solution)/shard_map/pallas_call | solution.py:379
  57.0 0.8 %shard_map.78 = (f32[2,128,128]{2,1,0:T(8,128)}, f32[2,2,256,128]{3,2,1,0:T(8,128)}) custom-call(f32[2,128,128]{2,1,0:T(8,128)S(1)} %get-tuple-element.6.obj_in, f32[2,2,256,128]{3,2,1,0:T(8,128)S(1)} %get-tuple-element.7.probe_in), custom_call_target="tpu_custom_call" | custom-call | tf_op jit(solution)/shard_map/pallas_call | solution.py:409

commit v3 on v2

--- a/solution.py
+++ b/solution.py
@@ -14,7 +14,6 @@
 BF16 = jnp.bfloat16
 CHUNKS = 2
 GROUP = 2
-UNROLL = 1
 
 
 def dft_parts(order):
@@ -133,68 +132,88 @@
     col_limit = jnp.where(pos < n_pos - 1, 2 * edge, edge)
     live = counts[0, 0]
 
-    def forward(slot, carry):
+    def crop_at(slot):
         row0, col0 = offsets[0, 0, slot], offsets[0, 1, slot]
         rows = one_hot((edge, 2 * edge), 1, row0, row_limit)
         cols = one_hot((2 * edge, edge), 0, col0, col_limit)
         lines = dot(rows, jnp.concatenate([window[0], window[1]], axis=1)).astype(BF16)
         crop = dot(jnp.concatenate([lines[:, : 2 * edge], lines[:, 2 * edge :]], axis=0), cols)
-        crop_r, crop_i = crop[:edge], crop[edge:]
-        crops[slot, 0], crops[slot, 1] = crop_r, crop_i
+        crops[slot, 0], crops[slot, 1] = crop[:edge], crop[edge:]
+
+    def rows_of(slot, m):
+        crop_r, crop_i = crops[slot, 0], crops[slot, 1]
+        exits = []
+        for n in range(m, m + GROUP):
+            probe_r, probe_i = probe[0, n], probe[1, n]
+            exits.append(
+                jnp.concatenate([probe_r * crop_r - probe_i * crop_i, probe_r * crop_i + probe_i * crop_r], axis=1)
+            )
+        half = on_right(split(jnp.concatenate(exits, axis=0)), tables.at[0])
+        for n in range(GROUP):
+            block = half[n * edge : (n + 1) * edge]
+            high, low = split(jnp.concatenate([block[:, :edge], block[:, edge:]], axis=0))
+            res_high[slot, m + n], res_low[slot, m + n] = high, low
+
+    def columns_of(slot, m):
+        picks = range(m, m + GROUP)
+        high = jnp.concatenate([res_high[slot, n] for n in picks], axis=1)
+        low = jnp.concatenate([res_low[slot, n] for n in picks], axis=1)
+        far = on_left(tables.at[1], (high, low))
+        return [far[:, n * edge : (n + 1) * edge] for n in range(GROUP)]
+
+    def residual(slot, fars):
         intensity = jnp.zeros((edge, edge), F32)
-        fars = []
-        for m in range(0, modes, GROUP):
-            exits = []
-            for n in range(m, m + GROUP):
-                probe_r, probe_i = probe[0, n], probe[1, n]
-                exits.append(
-                    jnp.concatenate([probe_r * crop_r - probe_i * crop_i, probe_r * crop_i + probe_i * crop_r], axis=1)
-                )
-            half = on_right(split(jnp.concatenate(exits, axis=0)), tables.at[0])
-            blocks = [half[n * edge : (n + 1) * edge] for n in range(GROUP)]
-            turned = jnp.concatenate(
-                [jnp.concatenate([block[:, :edge], block[:, edge:]], axis=0) for block in blocks], axis=1
-            )
-            far = on_left(tables.at[1], split(turned))
-            for n in range(GROUP):
-                part = far[:, n * edge : (n + 1) * edge]
-                intensity += part[:edge] * part[:edge] + part[edge:] * part[edge:]
-                fars.append(part)
+        for part in fars:
+            intensity += part[:edge] * part[:edge] + part[edge:] * part[edge:]
         factor = 1.0 - amp[0, slot] / jnp.sqrt(intensity + 1.0)
         factor = jnp.where(slot < live, factor, 0.0)
         factor = jnp.concatenate([factor, factor], axis=0)
         for m in range(modes):
             high, low = split(fars[m] * factor)
             res_high[slot, m], res_low[slot, m] = high, low
-        return carry
-
-    lax.fori_loop(0, slots, forward, 0, unroll=UNROLL)
+
+    for slot in range(slots):
+        crop_at(slot)
+    for m in range(0, modes, GROUP):
+        rows_of(0, m)
+    for slot in range(slots):
+        fars = []
+        for m in range(0, modes, GROUP):
+            if slot + 1 < slots:
+                rows_of(slot + 1, m)
+            fars += columns_of(slot, m)
+        residual(slot, fars)
 
     per = modes // CHUNKS
 
-    def backward_of(chunk):
-        def backward(slot, carry):
-            picks = range(chunk * per, (chunk + 1) * per)
-            high = jnp.concatenate([res_high[slot, m] for m in picks], axis=1)
-            low = jnp.concatenate([res_low[slot, m] for m in picks], axis=1)
-            half = on_left(tables.at[0], (high, low))
-            blocks = [half[:, n * edge : (n + 1) * edge] for n in range(per)]
-            turned = jnp.concatenate(
-                [jnp.concatenate([block[:edge], block[edge:]], axis=1) for block in blocks], axis=0
+    def back_columns(chunk, slot):
+        picks = range(chunk * per, (chunk + 1) * per)
+        high = jnp.concatenate([res_high[slot, m] for m in picks], axis=1)
+        low = jnp.concatenate([res_low[slot, m] for m in picks], axis=1)
+        half = on_left(tables.at[0], (high, low))
+        for n, m in enumerate(picks):
+            res_high[slot, m], res_low[slot, m] = split(half[:, n * edge : (n + 1) * edge])
+
+    def back_rows(chunk, slot):
+        parts = []
+        for ref in (res_high, res_low):
+            blocks = [ref[slot, m] for m in range(chunk * per, (chunk + 1) * per)]
+            parts.append(
+                jnp.concatenate([jnp.concatenate([block[:edge], block[edge:]], axis=1) for block in blocks], axis=0)
             )
-            back = on_right(split(turned), tables.at[1])
-            backs[slot, chunk] = back
-            crop_r, crop_i = crops[slot, 0], crops[slot, 1]
-            for n in range(per):
-                lines = slice(n * edge, (n + 1) * edge)
-                back_r, back_i = back[lines, :edge], back[lines, edge:]
-                term_r = crop_r * back_r + crop_i * back_i
-                term_i = crop_r * back_i - crop_i * back_r
+        back = on_right(parts, tables.at[1])
+        backs[slot, chunk] = back
+        crop_r, crop_i = crops[slot, 0], crops[slot, 1]
+        for n in range(per):
+            lines = slice(n * edge, (n + 1) * edge)
+            back_r, back_i = back[lines, :edge], back[lines, edge:]
+            term_r = crop_r * back_r + crop_i * back_i
+            term_i = crop_r * back_i - crop_i * back_r
+            if slot == 0:
+                terms[0, chunk, lines], terms[1, chunk, lines] = term_r, term_i
+            else:
                 terms[0, chunk, lines] += term_r
                 terms[1, chunk, lines] += term_i
-            return carry
-
-        return backward
 
     def place(slot):
         row0, col0 = offsets[0, 0, slot], offsets[0, 1, slot]
@@ -304,12 +323,16 @@
             to_core += sent([send(piece, piece, gc_send.at[q, s], gc_recv.at[q, s], sibling)])
         return to_core
 
-    terms[...] = jnp.zeros_like(terms)
-    lax.fori_loop(0, slots, backward_of(0), 0, unroll=UNROLL)
-    front = core_scatter(0)
-    lax.fori_loop(0, slots // 2, backward_of(1), 0, unroll=UNROLL)
-    front = x_scatter(0, front)
-    lax.fori_loop(slots // 2, slots, backward_of(1), 0, unroll=UNROLL)
+    units = [(chunk, slot) for chunk in range(CHUNKS) for slot in range(slots)]
+    back_columns(*units[0])
+    for this, following in zip(units, units[1:] + [None]):
+        if following:
+            back_columns(*following)
+        back_rows(*this)
+        if this == (0, slots - 1):
+            front = core_scatter(0)
+        if this == (1, slots // 2):
+            front = x_scatter(0, front)
     back = core_scatter(1)
     place(0)
     back = x_scatter(1, back)
@@ -379,7 +402,7 @@
         held = pl.pallas_call(
             functools.partial(kernel, sizes, scale),
             out_shape=(pltpu.VMEM((2, edge, edge), F32), pltpu.VMEM((2, CHUNKS, rows, edge), F32)),
-            in_specs=[any_space] * 6,
+            in_specs=[any_space] * 4 + [pl.BlockSpec(memory_space=pltpu.HBM), any_space],
             out_specs=(vmem_space, vmem_space),
             scratch_shapes=[
                 pltpu.SMEM((1, 2, slots), jnp.int32),

time: 58 us -> 53.8 us (0.928)
  Pallas kernels: 56.6 us -> 52.4 us
    pallas_call x1, Pallas kernels: 55.7 us -> 51.5 us  [on_device(): pl.pallas_call(functools.partial(kernel, sizes, scale), out_shape=(pltpu....]
where the time goes in v3:
time: 53.8 us; the launch traced here: 53.7 us
  Pallas kernels  52.4 us (97%)
  between operations  1.29 us (2%)
    pallas_call x1, Pallas kernels, on_device(): pl.pallas_call(functools.partial(kernel, sizes, scale), out_shape=(pltpu....  51.5 us

profile of v3, /device:TPU:1, one launch (start us, length us, event | category | flops | bytes accessed | tf_op | source)
XLA Modules:
  0.0 53.7 jit_solution(1203769166948523091)
XLA Ops:
  1.3 51.5 %shard_map.77 = (f32[2,128,128]{2,1,0:T(8,128)S(1)}, f32[2,2,256,128]{3,2,1,0:T(8,128)S(1)}) custom-call(bf16[2,128,128]{2,1,0:T(8,128)(2,1)} %tile.1, f32[2,4,128,128]{3,2,1,0:T(8,128)} %probe_h.1, f32[1,4,128,128]{3,2,1,0:T(8,128)} %amp_h.1, s32[1,2,4]{2,1,0:T(2,128)} %offsets_h.1, s32[1,1]{1,0:T(1,128)S(6)} %copy.8.counts_h, ...), custom_call_target="tpu_custom_call" | custom-call | tf_op jit(solution)/shard_map/pallas_call | solution.py:402
  52.8 0.8 %shard_map.78 = (f32[2,128,128]{2,1,0:T(8,128)}, f32[2,2,256,128]{3,2,1,0:T(8,128)}) custom-call(f32[2,128,128]{2,1,0:T(8,128)S(1)} %get-tuple-element.6.obj_in, f32[2,2,256,128]{3,2,1,0:T(8,128)S(1)} %get-tuple-element.7.probe_in), custom_call_target="tpu_custom_call" | custom-call | tf_op jit(solution)/shard_map/pallas_call | solution.py:432

commit v4 on v3

--- a/solution.py
+++ b/solution.py
@@ -13,20 +13,27 @@
 F32 = jnp.float32
 BF16 = jnp.bfloat16
 CHUNKS = 2
-GROUP = 2
+GROUP = 4
+
+
+def two_parts(table):
+    high = table.astype(np.float32).astype(jnp.bfloat16)
+    return high, (table - high.astype(np.float64)).astype(np.float32).astype(jnp.bfloat16)
 
 
 def dft_parts(order):
     index = np.arange(order)
     angle = (index[:, None] * index[None, :] % order) * (2.0 * math.pi / order)
     cos, sin = np.cos(angle) / math.sqrt(order), np.sin(angle) / math.sqrt(order)
-    right = np.block([[cos, -sin], [sin, cos]]).astype(np.float32)
-    parts = []
-    for table in (right, right.T):
-        high = table.astype(jnp.bfloat16)
-        low = (table - high.astype(np.float32)).astype(jnp.bfloat16)
-        parts.append(np.stack([high, low]))
-    return np.stack(parts)
+    right = np.block([[cos, -sin], [sin, cos]])
+    tables = [part for table in (right, right.T) for part in two_parts(table)]
+    for start in (0, 1):
+        c, s = cos[start::2, : order // 2], sin[start::2, : order // 2]
+        left = np.block([[c, s], [-s, c]])
+        for table in (left, left.T):
+            high, low = two_parts(table)
+            tables.append(np.block([[high, high], [low, low]]))
+    return np.stack(tables)
 
 
 def split(value):
@@ -39,18 +46,16 @@
 
 
 def on_left(table, value):
-    high, low = value
-    return dot(
-        jnp.concatenate([table[0], table[0], table[1]], axis=1),
-        jnp.concatenate([high, low, high], axis=0),
-    )
-
-
-def on_right(value, table):
+    both = dot(table[...], jnp.concatenate(value, axis=0))
+    rows = both.shape[0] // 2
+    return both[:rows] + both[rows:]
+
+
+def on_right(value, tables, at):
     high, low = value
     return dot(
         jnp.concatenate([high, low, high], axis=1),
-        jnp.concatenate([table[0], table[0], table[1]], axis=0),
+        jnp.concatenate([tables[at], tables[at], tables[at + 1]], axis=0),
     )
 
 
@@ -102,7 +107,7 @@
     loads = [
         pltpu.make_async_copy(offsets_h, offsets, load_sem.at[0]),
         pltpu.make_async_copy(counts_h, counts, load_sem.at[1]),
-        pltpu.make_async_copy(tile, window.at[:, first, first], load_sem.at[2]),
+        pltpu.make_async_copy(tile, window.at[0], load_sem.at[2]),
         pltpu.make_async_copy(probe_h, probe, load_sem.at[3]),
         pltpu.make_async_copy(tables_h, tables, load_sem.at[4]),
         pltpu.make_async_copy(amp_h, amp, load_sem.at[5]),
@@ -118,12 +123,14 @@
         copy.start()
         return copy
 
+    loads[2].wait()
+    mine = window.at[0]
     halo = [
-        send(tile, window.at[:, second, second], halo_send.at[0], halo_recv.at[0], (up, left)),
-        send(tile, window.at[:, first, second], halo_send.at[2], halo_recv.at[2], (region, left)),
-        send(tile, window.at[:, second, first], halo_send.at[1], halo_recv.at[1], (up, pos)),
+        send(mine, window.at[3], halo_send.at[0], halo_recv.at[0], (up, left)),
+        send(mine, window.at[1], halo_send.at[2], halo_recv.at[2], (region, left)),
+        send(mine, window.at[2], halo_send.at[1], halo_recv.at[1], (up, pos)),
     ]
-    for load in loads:
+    for load in loads[:2] + loads[3:]:
         load.wait()
     for copy in halo:
         copy.wait()
@@ -131,12 +138,17 @@
     row_limit = jnp.where(region < n_region - 1, 2 * edge, edge)
     col_limit = jnp.where(pos < n_pos - 1, 2 * edge, edge)
     live = counts[0, 0]
+    mid = edge // 2
 
     def crop_at(slot):
         row0, col0 = offsets[0, 0, slot], offsets[0, 1, slot]
         rows = one_hot((edge, 2 * edge), 1, row0, row_limit)
         cols = one_hot((2 * edge, edge), 0, col0, col_limit)
-        lines = dot(rows, jnp.concatenate([window[0], window[1]], axis=1)).astype(BF16)
+        field = jnp.concatenate(
+            [jnp.concatenate([window[k, part] for part in range(2) for k in pair], axis=1) for pair in ((0, 1), (2, 3))],
+            axis=0,
+        )
+        lines = dot(rows, field).astype(BF16)
         crop = dot(jnp.concatenate([lines[:, : 2 * edge], lines[:, 2 * edge :]], axis=0), cols)
         crops[slot, 0], crops[slot, 1] = crop[:edge], crop[edge:]
 
@@ -148,29 +160,31 @@
             exits.append(
                 jnp.concatenate([probe_r * crop_r - probe_i * crop_i, probe_r * crop_i + probe_i * crop_r], axis=1)
             )
-        half = on_right(split(jnp.concatenate(exits, axis=0)), tables.at[0])
+        half = on_right(split(jnp.concatenate(exits, axis=0)), tables, 0)
         for n in range(GROUP):
             block = half[n * edge : (n + 1) * edge]
-            high, low = split(jnp.concatenate([block[:, :edge], block[:, edge:]], axis=0))
-            res_high[slot, m + n], res_low[slot, m + n] = high, low
+            top = jnp.concatenate([block[:mid, :edge], block[:mid, edge:]], axis=0)
+            bottom = jnp.concatenate([block[mid:, :edge], block[mid:, edge:]], axis=0)
+            res_high[slot, 0, m + n], res_low[slot, 0, m + n] = split(top + bottom)
+            res_high[slot, 1, m + n], res_low[slot, 1, m + n] = split(top - bottom)
+
+    def halves(slot, kind, picks):
+        return [jnp.concatenate([ref[slot, kind, n] for n in picks], axis=1) for ref in (res_high, res_low)]
 
     def columns_of(slot, m):
-        picks = range(m, m + GROUP)
-        high = jnp.concatenate([res_high[slot, n] for n in picks], axis=1)
-        low = jnp.concatenate([res_low[slot, n] for n in picks], axis=1)
-        far = on_left(tables.at[1], (high, low))
-        return [far[:, n * edge : (n + 1) * edge] for n in range(GROUP)]
+        fars = [on_left(tables.at[4 + 2 * kind], halves(slot, kind, range(m, m + GROUP))) for kind in range(2)]
+        return [[far[:, n * edge : (n + 1) * edge] for far in fars] for n in range(GROUP)]
 
     def residual(slot, fars):
-        intensity = jnp.zeros((edge, edge), F32)
-        for part in fars:
-            intensity += part[:edge] * part[:edge] + part[edge:] * part[edge:]
-        factor = 1.0 - amp[0, slot] / jnp.sqrt(intensity + 1.0)
-        factor = jnp.where(slot < live, factor, 0.0)
-        factor = jnp.concatenate([factor, factor], axis=0)
-        for m in range(modes):
-            high, low = split(fars[m] * factor)
-            res_high[slot, m], res_low[slot, m] = high, low
+        for kind in range(2):
+            intensity = jnp.zeros((mid, edge), F32)
+            for far in fars:
+                intensity += far[kind][:mid] * far[kind][:mid] + far[kind][mid:] * far[kind][mid:]
+            factor = 1.0 - amp[0, slot, pl.ds(kind, mid, stride=2)] / jnp.sqrt(intensity + 1.0)
+            factor = jnp.where(slot < live, factor, 0.0)
+            factor = jnp.concatenate([factor, factor], axis=0)
+            for m in range(modes):
+                res_high[slot, kind, m], res_low[slot, kind, m] = split(fars[m][kind] * factor)
 
     for slot in range(slots):
         crop_at(slot)
@@ -188,20 +202,19 @@
 
     def back_columns(chunk, slot):
         picks = range(chunk * per, (chunk + 1) * per)
-        high = jnp.concatenate([res_high[slot, m] for m in picks], axis=1)
-        low = jnp.concatenate([res_low[slot, m] for m in picks], axis=1)
-        half = on_left(tables.at[0], (high, low))
-        for n, m in enumerate(picks):
-            res_high[slot, m], res_low[slot, m] = split(half[:, n * edge : (n + 1) * edge])
+        even, odd = (on_left(tables.at[5 + 2 * kind], halves(slot, kind, picks)) for kind in range(2))
+        for kind, half in enumerate((even + odd, even - odd)):
+            for n, m in enumerate(picks):
+                res_high[slot, kind, m], res_low[slot, kind, m] = split(half[:, n * edge : (n + 1) * edge])
 
     def back_rows(chunk, slot):
         parts = []
         for ref in (res_high, res_low):
-            blocks = [ref[slot, m] for m in range(chunk * per, (chunk + 1) * per)]
+            blocks = [ref[slot, kind, m] for m in range(chunk * per, (chunk + 1) * per) for kind in range(2)]
             parts.append(
-                jnp.concatenate([jnp.concatenate([block[:edge], block[edge:]], axis=1) for block in blocks], axis=0)
+                jnp.concatenate([jnp.concatenate([block[:mid], block[mid:]], axis=1) for block in blocks], axis=0)
             )
-        back = on_right(parts, tables.at[1])
+        back = on_right(parts, tables, 2)
         backs[slot, chunk] = back
         crop_r, crop_i = crops[slot, 0], crops[slot, 1]
         for n in range(per):
@@ -360,6 +373,9 @@
     total += jnp.where(jnp.logical_and(region > 0, pos > 0), from_grad[0], 0.0)
     obj_out[...] = total
     back = x_gather(1, back)
+    for copy in pending:
+        copy.wait_send()
+    pending.clear()
     front = core_gather(0, front)
     back = core_gather(1, back)
     for copy in front + back:
@@ -407,13 +423,13 @@
             scratch_shapes=[
                 pltpu.SMEM((1, 2, slots), jnp.int32),
                 pltpu.SMEM((1, 1), jnp.int32),
-                pltpu.VMEM((2, 2 * edge, 2 * edge), BF16),
+                pltpu.VMEM((4, 2, edge, edge), BF16),
                 pltpu.VMEM((2, modes, edge, edge), F32),
                 pltpu.VMEM((1, slots, edge, edge), F32),
-                pltpu.VMEM((2, 2, 2 * edge, 2 * edge), BF16),
+                pltpu.VMEM((8, 2 * edge, 2 * edge), BF16),
                 pltpu.VMEM((slots, 2, edge, edge), F32),
-                pltpu.VMEM((slots, modes, 2 * edge, edge), BF16),
-                pltpu.VMEM((slots, modes, 2 * edge, edge), BF16),
+                pltpu.VMEM((slots, 2, modes, edge, edge), BF16),
+                pltpu.VMEM((slots, 2, modes, edge, edge), BF16),
                 pltpu.VMEM((slots, CHUNKS, rows, 2 * edge), F32),
                 pltpu.VMEM((2, 2 * edge, 2 * edge), F32),
                 pltpu.VMEM((2, CHUNKS, rows, edge), F32),

time: 53.8 us -> 53.2 us (0.989)
  Pallas kernels: 52.4 us -> 51.8 us
    pallas_call x1, Pallas kernels: 51.5 us -> 51 us  [on_device(): pl.pallas_call(functools.partial(kernel, sizes, scale), out_shape=(pltpu....]
where the time goes in v4:
time: 53.2 us; the launch traced here: 53.1 us
  Pallas kernels  51.8 us (97%)
  between operations  1.29 us (2%)
    pallas_call x1, Pallas kernels, on_device(): pl.pallas_call(functools.partial(kernel, sizes, scale), out_shape=(pltpu....  51 us

profile of v4, /device:TPU:1, one launch (start us, length us, event | category | flops | bytes accessed | tf_op | source)
XLA Modules:
  0.0 53.1 jit_solution(9428253740615190540)
XLA Ops:
  1.3 51.0 %shard_map.77 = (f32[2,128,128]{2,1,0:T(8,128)S(1)}, f32[2,2,256,128]{3,2,1,0:T(8,128)S(1)}) custom-call(bf16[2,128,128]{2,1,0:T(8,128)(2,1)} %tile.1, f32[2,4,128,128]{3,2,1,0:T(8,128)} %probe_h.1, f32[1,4,128,128]{3,2,1,0:T(8,128)} %amp_h.1, s32[1,2,4]{2,1,0:T(2,128)} %offsets_h.1, s32[1,1]{1,0:T(1,128)S(6)} %copy.8.counts_h, ...), custom_call_target="tpu_custom_call" | custom-call | tf_op jit(solution)/shard_map/pallas_call | solution.py:418
  52.2 0.8 %shard_map.78 = (f32[2,128,128]{2,1,0:T(8,128)}, f32[2,2,256,128]{3,2,1,0:T(8,128)}) custom-call(f32[2,128,128]{2,1,0:T(8,128)S(1)} %get-tuple-element.6.obj_in, f32[2,2,256,128]{3,2,1,0:T(8,128)S(1)} %get-tuple-element.7.probe_in), custom_call_target="tpu_custom_call" | custom-call | tf_op jit(solution)/shard_map/pallas_call | solution.py:448

commit v5 on v4

--- a/solution.py
+++ b/solution.py
@@ -96,7 +96,7 @@
     def at_z(step):
         return (lax.rem(z + step, nz) * 2 + core, pos)
 
-    partners = [(down, right), (down, pos), (region, right), (up, left), (up, pos), (region, left), sibling]
+    partners = [(down, right), (down, pos), (region, right), (up, left), (up, pos), (region, left)]
     partners += [at_z(s) for s in by_distance(nz)] + [at_y(s) for s in by_distance(ny)]
     partners += [at_x(s) for s in by_distance(nx)]
     barrier = pltpu.get_barrier_semaphore()
@@ -365,6 +365,7 @@
     front = y_gather(0, front)
     back = y_gather(1, back)
     front = x_gather(0, front)
+    back = x_gather(1, back)
     for copy in grad_copies:
         copy.wait()
     total = grads[:, first, first]
@@ -372,7 +373,6 @@
     total += jnp.where(region > 0, from_grad[1], 0.0)
     total += jnp.where(jnp.logical_and(region > 0, pos > 0), from_grad[0], 0.0)
     obj_out[...] = total
-    back = x_gather(1, back)
     for copy in pending:
         copy.wait_send()
     pending.clear()

time: 53.2 us -> 53.2 us (level)
  no operation moved by 1% of the time
where the time goes in v5:
time: 53.2 us; the launch traced here: 53.1 us
  Pallas kernels  51.8 us (97%)
  between operations  1.29 us (2%)
    pallas_call x1, Pallas kernels, on_device(): pl.pallas_call(functools.partial(kernel, sizes, scale), out_shape=(pltpu....  51 us

profile of v5, /device:TPU:1, one launch (start us, length us, event | category | flops | bytes accessed | tf_op | source)
XLA Modules:
  0.0 53.1 jit_solution(6757847234006148598)
XLA Ops:
  1.3 51.0 %shard_map.77 = (f32[2,128,128]{2,1,0:T(8,128)S(1)}, f32[2,2,256,128]{3,2,1,0:T(8,128)S(1)}) custom-call(bf16[2,128,128]{2,1,0:T(8,128)(2,1)} %tile.1, f32[2,4,128,128]{3,2,1,0:T(8,128)} %probe_h.1, f32[1,4,128,128]{3,2,1,0:T(8,128)} %amp_h.1, s32[1,2,4]{2,1,0:T(2,128)} %offsets_h.1, s32[1,1]{1,0:T(1,128)S(6)} %copy.8.counts_h, ...), custom_call_target="tpu_custom_call" | custom-call | tf_op jit(solution)/shard_map/pallas_call | solution.py:418
  52.2 0.8 %shard_map.78 = (f32[2,128,128]{2,1,0:T(8,128)}, f32[2,2,256,128]{3,2,1,0:T(8,128)}) custom-call(f32[2,128,128]{2,1,0:T(8,128)S(1)} %get-tuple-element.6.obj_in, f32[2,2,256,128]{3,2,1,0:T(8,128)S(1)} %get-tuple-element.7.probe_in), custom_call_target="tpu_custom_call" | custom-call | tf_op jit(solution)/shard_map/pallas_call | solution.py:448
